TPU v7x, 32 devices: a whole 2x2x4 slice. The times are simulated.
32 devices in a mesh: group: 1, tile: 8 (over z, core), dp: 4 (over y, x).
Axes of the slice: x: 2, y: 2, z: 4, core: 2. Of those that a mesh axis runs over, the one named last changes fastest.
Arguments:
- activations: bfloat16 [4, 8, 24, 24, 128], P(('group', 'dp'), 'tile'), may hold values from -6 to 6
- cotangent: bfloat16 [4, 8, 24, 24, 128], P(('group', 'dp'), 'tile'), may hold values from -1.5 to 1.5
- kernel: bfloat16 [1152, 128], P('group'), may hold values from -0.1875 to 0.1875
- turning: int32 [8], P('tile'), may hold values from 0 to 3
- orient: int32 [8, 4], P('tile'), may hold values from 0 to 7, as said below
- left_factor: float32 [1152, 1152], P(('group', 'tile')), may hold values from -0.15 to 5.15
- left_basis: float32 [1152, 1152], P(('group', 'tile'), 'dp'), may hold values from -0.026516504 to 1.0265165
- right_factor: float32 [128, 128], P('group'), may hold values from -4.26 to 49.26
- right_basis: float32 [128, 128], P('group'), may hold values from -0.079549513 to 1.0795495
- momentum: float32 [1152, 128], P(('group', 'dp')), may hold values from -1.5 to 1.5
- second_moment: float32 [1152, 128], P(('group', 'dp')), may hold values from 0.02 to 0.2
Outputs:
- output: bfloat16 [4, 8, 24, 24, 128], P(('group', 'dp'), 'tile')
- input_grad: bfloat16 [4, 8, 24, 24, 128], P(('group', 'dp'), 'tile')
- kernel_grad: float32 [1152, 128], P('group')
- left_factor_new: float32 [1152, 1152], P(('group', 'tile'))
- left_basis_new: float32 [1152, 1152], P(('group', 'tile'))
- right_factor_new: float32 [128, 128], P('group')
- right_basis_new: float32 [128, 128], P('group')
- momentum_new: float32 [1152, 128], P(('group', 'dp'))
- second_new: float32 [1152, 128], P(('group', 'dp'))
- update: float32 [1152, 128], P(('group', 'tile'))
Inputs may be any that keep to these rules, and one draw needn't show every extreme that they name: 0 where edge e of tile t leaves the patch; otherwise orient[t, e] % 4 is the edge of neighbor[t, e] that heads back to t, and 4 is added where the two edges' cell orders run opposite ways.
All inputs are finite; a program needn't handle non-finite values.
Results may differ from a plain program's by a relative error of at most 0.0025.
Values may be sent and summed in bfloat16 or wider, within the bound.
A program may use at most 128 MiB of HBM per device.

v0:
```python
import math
import jax
import jax.numpy as jnp
from jax import lax
from jax.sharding import PartitionSpec as P

highest = lax.Precision.HIGHEST
epsilon = 1e-08


def edge_strips(values):
    return jnp.stack(
        [values[..., 0, :, :], values[..., :, -1, :], values[..., -1, :, :], values[..., :, 0, :]],
        axis=0,
    )


def cycle_strips(spread):
    return jnp.stack(
        [spread[:, 0, 1:-1], spread[:, 1:-1, -1], spread[:, -1, 1:-1], spread[:, 1:-1, 0]], axis=0
    )


def assemble(tile_vals, borders):
    middle = jnp.concatenate(
        [borders[3][:, :, None, :], tile_vals, borders[1][:, :, None, :]], axis=2
    )
    top_row = jnp.pad(borders[0], ((0, 0), (1, 1), (0, 0)))[:, None]
    bottom_row = jnp.pad(borders[2], ((0, 0), (1, 1), (0, 0)))[:, None]
    return jnp.concatenate([top_row, middle, bottom_row], axis=1)


def tap_patches(padded, side):
    pieces = [
        padded[:, row_off : row_off + side, col_off : col_off + side, :]
        for row_off in range(3)
        for col_off in range(3)
    ]
    joined = jnp.concatenate(pieces, axis=-1)
    return joined.reshape(-1, joined.shape[-1])


def spread_back(flat_grads, kernel, sample_count, side):
    channels = kernel.shape[1]
    summed = jnp.zeros((sample_count, side + 2, side + 2, channels), jnp.float32)
    for tap_index in range(9):
        row_off, col_off = divmod(tap_index, 3)
        weight_tap = kernel[tap_index * channels : (tap_index + 1) * channels]
        contrib = lax.dot_general(
            flat_grads, weight_tap, (((1,), (1,)), ((), ())), preferred_element_type=jnp.float32
        )
        contrib = contrib.reshape(sample_count, side, side, channels)
        summed = summed + jnp.pad(
            contrib, ((0, 0), (row_off, 2 - row_off), (col_off, 2 - col_off), (0, 0))
        )
    return summed


def absorb_rims(interior, incoming):
    result = interior.at[..., 0, :, :].add(incoming[0])
    result = result.at[..., :, -1, :].add(incoming[1])
    result = result.at[..., -1, :, :].add(incoming[2])
    return result.at[..., :, 0, :].add(incoming[3])


def flip_edges(strips, flipped):
    return jnp.where(flipped[:, None, None, None], strips[:, :, ::-1, :], strips)


def pick_gathered(everything, near_tiles, facing, flipped, usable):
    flat = everything.reshape(everything.shape[0] * 4, -1)
    wanted = jnp.where(usable, near_tiles * 4 + facing, -1)
    selector = (lax.broadcasted_iota(jnp.int32, (4, flat.shape[0]), 1) == wanted[:, None]).astype(
        jnp.bfloat16
    )
    picked = jnp.dot(selector, flat, preferred_element_type=jnp.float32).astype(jnp.bfloat16)
    return flip_edges(picked.reshape((4,) + everything.shape[2:]), flipped)


def orthonormal(power):
    gram = lax.dot_general(power, power, (((0,), (0,)), ((), ())), precision=highest)
    lower = jnp.linalg.cholesky(gram)
    return lax.linalg.triangular_solve(lower, power.T, left_side=True, lower=True).T


def body(
    activations,
    cotangent,
    kernel,
    turning,
    orient,
    left_factor,
    left_basis,
    right_factor,
    right_basis,
    momentum,
    second_moment,
):
    tiles = lax.axis_size("tile")
    dp_count = lax.axis_size("dp")
    tile_index = lax.axis_index("tile")
    dp_index = lax.axis_index("dp")
    tile_vals = activations[:, 0]
    tile_grads = cotangent[:, 0]
    sample_count = tile_vals.shape[0]
    side = tile_vals.shape[1]
    channels = tile_vals.shape[-1]
    own_turn = turning[0]
    facing = orient[0] % 4
    flipped = orient[0] >= 4
    heading = (jnp.arange(4, dtype=jnp.int32) + own_turn) % 4
    row_of = tile_index // 4
    col_of = tile_index % 4
    room = jnp.stack([row_of > 0, col_of < 3, row_of < tiles // 4 - 1, col_of > 0])
    usable = (
        jnp.sum(
            jnp.where(
                heading[:, None] == jnp.arange(4, dtype=jnp.int32)[None, :], room[None, :], False
            ),
            axis=1,
        )
        > 0
    )
    offsets = jnp.array([-4, 1, 4, -1], dtype=jnp.int32)
    near_tiles = tile_index + jnp.sum(
        jnp.where(heading[:, None] == jnp.arange(4, dtype=jnp.int32)[None, :], offsets[None, :], 0),
        axis=1,
    )
    strips = edge_strips(tile_vals)
    everything = lax.all_gather(strips[None], "tile", axis=0, tiled=True)
    borders = pick_gathered(everything, near_tiles, facing, flipped, usable)
    padded = assemble(tile_vals, borders)
    columns = tap_patches(padded, side)
    flat_grads = tile_grads.reshape(-1, channels)
    partial_grad = lax.dot_general(
        columns, flat_grads, (((0,), (0,)), ((), ())), preferred_element_type=jnp.float32
    )
    summed_grad = lax.psum(partial_grad, ("tile", "dp"))
    result = jnp.dot(columns, kernel, preferred_element_type=jnp.float32).astype(jnp.bfloat16)
    result = result.reshape(activations.shape)
    spread = spread_back(flat_grads, kernel, sample_count, side)
    rim_cells = cycle_strips(spread).astype(jnp.bfloat16)
    all_rims = lax.all_gather(rim_cells[None], "tile", axis=0, tiled=True)
    incoming = pick_gathered(all_rims, near_tiles, facing, flipped, usable)
    input_grad = absorb_rims(spread[:, 1:-1, 1:-1], incoming.astype(jnp.float32)).astype(
        jnp.bfloat16
    )
    input_grad = input_grad.reshape(cotangent.shape)
    cells = dp_count * sample_count * tiles * side * side
    grad = summed_grad * (1.0 / math.sqrt(cells))
    rows_per = left_factor.shape[0]
    width = left_factor.shape[1]
    cols_per = left_basis.shape[1]
    col_start = dp_index * cols_per
    grad_rows = lax.dynamic_slice_in_dim(grad, tile_index * rows_per, rows_per, 0)
    left_new = 0.95 * left_factor + 0.05 * lax.dot_general(
        grad_rows, grad, (((1,), (1,)), ((), ())), precision=highest
    )
    basis_rows = lax.all_gather(left_basis, "dp", axis=1, tiled=True)
    power = jnp.zeros((rows_per, width), jnp.float32) + jnp.dot(
        left_new,
        lax.all_gather(basis_rows.astype(jnp.bfloat16), "tile", axis=0, tiled=True).astype(
            jnp.float32
        ),
        precision=highest,
    )
    power_cols = lax.dynamic_slice_in_dim(power, col_start, cols_per, 1)
    gram_part = lax.psum(
        lax.dot_general(power, power_cols, (((0,), (0,)), ((), ())), precision=highest), "tile"
    )
    gram = lax.all_gather(gram_part, "dp", axis=1, tiled=True)
    lower = jnp.linalg.cholesky(gram)
    basis_new = lax.linalg.triangular_solve(lower, power.T, left_side=True, lower=True).T
    right_new = 0.95 * right_factor + 0.05 * lax.dot_general(
        grad, grad, (((0,), (0,)), ((), ())), precision=highest
    )
    right_basis_new = orthonormal(jnp.dot(right_new, right_basis, precision=highest))
    back = lax.psum(jnp.dot(left_basis, momentum, precision=highest), "dp")
    basis_cols = lax.dynamic_slice_in_dim(basis_new, col_start, cols_per, 1)
    turned_momentum, turned_grad = lax.psum(
        (
            lax.dot_general(basis_cols, back, (((0,), (0,)), ((), ())), precision=highest),
            lax.dot_general(basis_cols, grad_rows, (((0,), (0,)), ((), ())), precision=highest),
        ),
        "tile",
    )
    right_turn = lax.dot_general(
        right_basis, right_basis_new, (((0,), (0,)), ((), ())), precision=highest
    )
    rotated = jnp.dot(turned_momentum, right_turn, precision=highest)
    projected = jnp.dot(turned_grad, right_basis_new, precision=highest)
    momentum_new = 0.9 * rotated + 0.1 * projected
    second_new = 0.95 * second_moment + 0.05 * projected * projected
    normalized = momentum_new / (jnp.sqrt(second_new) + epsilon)
    whole_moment = lax.all_gather(normalized, "dp", axis=0, tiled=True)
    update_rows = jnp.dot(basis_new, whole_moment, precision=highest)
    update = lax.dot_general(
        update_rows, right_basis_new, (((1,), (1,)), ((), ())), precision=highest
    )
    return (
        result,
        input_grad,
        grad,
        left_new,
        basis_new,
        right_new,
        right_basis_new,
        momentum_new,
        second_new,
        update,
    )


def solution(mesh):
    placed = (
        P(("group", "dp"), "tile", None, None, None),
        P(("group", "dp"), "tile", None, None, None),
        P("group", None),
        P("tile"),
        P("tile", None),
        P(("group", "tile"), None),
        P(("group", "tile"), "dp"),
        P("group", None),
        P("group", None),
        P(("group", "dp"), None),
        P(("group", "dp"), None),
    )
    return jax.shard_map(
        body,
        mesh=mesh,
        in_specs=placed,
        out_specs=(
            P(("group", "dp"), "tile", None, None, None),
            P(("group", "dp"), "tile", None, None, None),
            P("group", None),
            P(("group", "tile"), None),
            P(("group", "tile"), None),
            P("group", None),
            P("group", None),
            P(("group", "dp"), None),
            P(("group", "dp"), None),
            P(("group", "tile"), None),
        ),
        check_vma=False,
    )
```

profile of v0, /device:TPU:0, one launch (start us, length us, event | category | flops | bytes accessed | tf_op | source)
XLA Modules:
  0.0 795.9 jit_solution(18225096363000132094)
XLA Ops:
  19.2 15.8 %all_gather.19 = bf16[8,4,1,24,128]{4,3,2,1,0:T(8,128)(2,1)S(1)} all-gather(bf16[1,4,1,24,128]{4,3,2,1,0:T(8,128)(2,1)S(1)} %pad_maximum_fusion.4), channel_id=1, replica_groups=mesh['group'=1,'tile'=8,'dp'=4] {'tile'}, dimensions={0}, use_global_device_ids=true | all-gather | bytes 221184 | tf_op jit(solution)/shard_map/all_gather | solution.py:143
  36.3 14.1 %all-gather = bf16[32,1,24,128]{3,2,1,0:T(8,128)(2,1)S(1)} all-gather(bf16[4,1,24,128]{3,2,1,0:T(8,128)(2,1)S(1)} %pad_maximum_fusion.3), channel_id=2, replica_groups=mesh['group'=1,'tile'=8,'dp'=4] {'tile'}, dimensions={0}, use_global_device_ids=true | all-gather | bytes 221184 | tf_op jit(solution)/shard_map/all_gather | solution.py:130
  53.1 10.2 %all-gather.1 = bf16[4,288,144]{1,2,0:T(8,128)(2,1)S(1)} all-gather(bf16[1,288,144]{1,2,0:T(8,128)(2,1)S(1)} %bitcast_convert_fusion), channel_id=1, replica_groups=mesh['group'=1,'tile'=8,'dp'=4] {'dp'}, dimensions={0}, use_global_device_ids=true | all-gather | bytes 414720 | tf_op jit(solution)/shard_map/all_gather | solution.py:159
  64.7 132.0 %all-reduce.18.cloned.1.call-done = f32[1152,128]{1,0:T(8,128)} async-done(((f32[1152,128]{1,0:T(8,128)}), f32[1152,128]{1,0:T(8,128)}) %all-reduce.18.cloned.1.call-update) | async-done | bytes 589840 | tf_op jit(solution)/shard_map/psum | solution.py:138
  206.1 60.6 %all-reduce.20.cloned.1.call-done = f32[1152,288]{0,1:T(8,128)} async-done(((f32[1152,288]{0,1:T(8,128)}), f32[1152,288]{0,1:T(8,128)}) %all-reduce.20.cloned.1.call-update) | async-done | bytes 1327120 | tf_op jit(solution)/shard_map/psum | solution.py:168
  276.5 11.7 %cholesky.693 = f32[128,128]{1,0:T(8,128)S(1)} custom-call(f32[128,128]{1,0:T(8,128)S(1)} %fusion.98), custom_call_target="Cholesky" | custom-call | tf_op jit(solution)/shard_map/jit(cholesky)/cholesky | solution.py:82
  289.6 9.8 %custom-call.85 = f32[1,128,128]{1,2,0:T(8,128)S(1)} custom-call(f32[1,128,128]{2,1,0:T(8,128)S(1)} %fusion.85), custom_call_target="InvertDiagBlocksLowerTriangular" | custom-call | tf_op jit(solution)/shard_map/triangular_solve | solution.py:83
  300.4 28.1 %all-gather.7.cloned.1.call-done = f32[1152,1152]{0,1:T(8,128)} async-done(((f32[1152,288]{0,1:T(8,128)}), f32[1152,1152]{0,1:T(8,128)}) %all-gather.7.cloned.1.call-update) | async-done | bytes 5308432 | tf_op jit(solution)/shard_map/all_gather | solution.py:171
  342.7 11.7 %cholesky.273 = f32[128,128]{1,0:T(8,128)S(1)} custom-call(f32[128,128]{1,0:T(8,128)S(1)} %cholesky.705), custom_call_target="Cholesky" | custom-call | tf_op jit(solution)/shard_map/jit(cholesky)/cholesky | solution.py:172
  357.1 9.8 %custom-call.76 = f32[1,128,128]{1,2,0:T(8,128)S(1)} custom-call(f32[1,128,128]{2,1,0:T(8,128)S(1)} %get-tuple-element.210), custom_call_target="InvertDiagBlocksLowerTriangular" | custom-call | tf_op jit(solution)/shard_map/jit(cholesky)/cholesky | solution.py:172
  371.1 11.7 %cholesky.294 = f32[128,128]{1,0:T(8,128)S(1)} custom-call(f32[128,128]{1,0:T(8,128)S(1)} %cholesky.709), custom_call_target="Cholesky" | custom-call | tf_op jit(solution)/shard_map/jit(cholesky)/cholesky | solution.py:172
  383.5 10.0 %custom-call.77 = f32[1,128,128]{1,2,0:T(8,128)S(1)} custom-call(f32[1,128,128]{2,1,0:T(8,128)S(1)} %get-tuple-element.207), custom_call_target="InvertDiagBlocksLowerTriangular" | custom-call | tf_op jit(solution)/shard_map/jit(cholesky)/cholesky | solution.py:172
  397.1 11.7 %cholesky.321 = f32[128,128]{1,0:T(8,128)S(1)} custom-call(f32[128,128]{1,0:T(8,128)S(1)} %cholesky.714), custom_call_target="Cholesky" | custom-call | tf_op jit(solution)/shard_map/jit(cholesky)/cholesky | solution.py:172
  423.2 11.9 %cholesky.583 = f32[128,128]{1,0:T(8,128)S(1)} custom-call(f32[128,128]{1,0:T(8,128)S(1)} %cholesky.719), custom_call_target="Cholesky" | custom-call | tf_op jit(solution)/shard_map/jit(cholesky)/cholesky | solution.py:172
  449.3 11.7 %cholesky.602 = f32[128,128]{1,0:T(8,128)S(1)} custom-call(f32[128,128]{1,0:T(8,128)S(1)} %cholesky.724), custom_call_target="Cholesky" | custom-call | tf_op jit(solution)/shard_map/jit(cholesky)/cholesky | solution.py:172
  461.7 10.2 %custom-call.80 = f32[1,128,128]{1,2,0:T(8,128)S(1)} custom-call(f32[1,128,128]{2,1,0:T(8,128)S(1)} %get-tuple-element.198), custom_call_target="InvertDiagBlocksLowerTriangular" | custom-call | tf_op jit(solution)/shard_map/jit(cholesky)/cholesky | solution.py:172
  475.8 11.7 %cholesky.622 = f32[128,128]{1,0:T(8,128)S(1)} custom-call(f32[128,128]{1,0:T(8,128)S(1)} %cholesky.729), custom_call_target="Cholesky" | custom-call | tf_op jit(solution)/shard_map/jit(cholesky)/cholesky | solution.py:172
  501.6 11.9 %cholesky.642 = f32[128,128]{1,0:T(8,128)S(1)} custom-call(f32[128,128]{1,0:T(8,128)S(1)} %cholesky.734), custom_call_target="Cholesky" | custom-call | tf_op jit(solution)/shard_map/jit(cholesky)/cholesky | solution.py:172
  527.1 11.7 %cholesky.662 = f32[128,128]{1,0:T(8,128)S(1)} custom-call(f32[128,128]{1,0:T(8,128)S(1)} %cholesky.739), custom_call_target="Cholesky" | custom-call | tf_op jit(solution)/shard_map/jit(cholesky)/cholesky | solution.py:172
  551.9 11.9 %cholesky.680 = f32[128,128]{1,0:T(8,128)S(1)} custom-call(f32[128,128]{1,0:T(8,128)S(1)} %convolution_subtract_fusion.12), custom_call_target="Cholesky" | custom-call | tf_op jit(solution)/shard_map/jit(cholesky)/cholesky | solution.py:172
  581.3 31.4 %while.5 = (s32[]{:T(128)}, f32[1152,1152]{1,0:T(8,128)}, s32[9,2]{0,1:T(2,128)S(1)}, f32[9,128,128]{2,1,0:T(8,128)}, s32[]{:T(128)}) while((s32[]{:T(128)}, f32[1152,1152]{1,0:T(8,128)}, s32[9,2]{0,1:T(2,128)S(1)}, f32[9,128,128]{2,1,0:T(8,128)}, s32[]{:T(128)}) %tuple.112), condition=%wide.while_cond.4, body=%wide.while_body.4.sunk | while | flops 2 | bytes 132205 | solution.py:173
  612.8 89.2 %custom-call.84 = f32[9,128,128]{1,2,0:T(8,128)S(1)} custom-call(f32[9,128,128]{2,1,0:T(8,128)} %get-tuple-element.65), custom_call_target="InvertDiagBlocksLowerTriangular" | custom-call | tf_op jit(solution)/shard_map/triangular_solve | solution.py:173
  719.5 52.8 %all-reduce.24.cloned.1.call-done = (f32[288,128]{1,0:T(8,128)}, f32[288,128]{1,0:T(8,128)}) async-done(((f32[288,128]{1,0:T(8,128)}, f32[288,128]{1,0:T(8,128)}), (f32[288,128]{1,0:T(8,128)}, f32[288,128]{1,0:T(8,128)})) %all-reduce.24.cloned.1.call-update) | async-done | bytes 294928 | tf_op jit(solution)/shard_map/psum | solution.py:180
  775.4 11.2 %all_gather.23 = f32[1152,128]{1,0:T(8,128)S(1)} all-gather(f32[288,128]{1,0:T(8,128)S(1)} %get-tuple-element.128), channel_id=1, replica_groups=mesh['group'=1,'tile'=8,'dp'=4] {'dp'}, dimensions={0}, use_global_device_ids=true | all-gather | bytes 737280 | tf_op jit(solution)/shard_map/all_gather | solution.py:195
  (221 shorter events, 201.5 us)
Async XLA Ops:
  8.0 1.0 copy-start
  8.0 27.8 %copy-start.11 = (s32[4]{0:T(128)S(1)}, s32[4]{0:T(128)}, u32[]{:S(2)}) copy-start(s32[4]{0:T(128)} %constant.530.clone) | copy-start | bytes 52
  8.0 11.1 %copy-start.5 = (bf16[1,1,24,24,128]{4,3,2,1,0:T(8,128)(2,1)S(1)}, bf16[1,1,24,24,128]{4,3,2,1,0:T(8,128)(2,1)}, u32[]{:S(2)}) copy-start(bf16[1,1,24,24,128]{4,3,2,1,0:T(8,128)(2,1)} %param.20) | copy-start | bytes 442372
  8.0 27.6 %copy-start.10 = (s32[1,4]{1,0:T(1,128)S(1)}, s32[1,4]{1,0:T(1,128)}, u32[]{:S(2)}) copy-start(s32[1,4]{1,0:T(1,128)} %param.24) | copy-start | bytes 52
  8.1 188.6 %all-reduce.18.cloned.1.call-start = ((), (), s32[]{:S(2)}) async-start(), calls=%async_computation | async-start | bytes 1179648 | tf_op jit(solution)/shard_map/psum | solution.py:138
  19.0 34.1 %copy-start.6 = (f32[144,288]{1,0:T(8,128)S(1)}, f32[144,288]{1,0:T(8,128)}, u32[]{:S(2)}) copy-start(f32[144,288]{1,0:T(8,128)} %param.26) | copy-start | bytes 497668
  53.1 146.8 %all-gather.5.cloned.1.call-start = ((), (), s32[]{:S(2)}) async-start(), calls=%async_computation.1 | async-start | bytes 2985984 | tf_op jit(solution)/shard_map/all_gather | solution.py:162
  64.6 202.1 %all-reduce.20.cloned.1.call-start = ((), (), s32[]{:S(2)}) async-start(), calls=%async_computation.2 | async-start | bytes 2654208 | tf_op jit(solution)/shard_map/psum | solution.py:168
  197.8 517.7 %copy-start.2 = (f32[1152,128]{1,0:T(8,128)}, f32[1152,128]{1,0:T(8,128)S(1)}, u32[]{:S(2)}) copy-start(f32[1152,128]{1,0:T(8,128)S(1)} %broadcast_multiply_fusion) | copy-start | bytes 1769476
  199.8 71.1 %copy-start.3 = (f32[144,1152]{1,0:T(8,128)}, f32[144,1152]{1,0:T(8,128)S(1)}, u32[]{:S(2)}) copy-start(f32[144,1152]{1,0:T(8,128)S(1)} %fusion.1) | copy-start | bytes 1990660
  203.4 72.4 %copy-start.7 = (f32[128,128]{1,0:T(8,128)S(1)}, f32[128,128]{1,0:T(8,128)}, u32[]{:S(2)}) copy-start(f32[128,128]{1,0:T(8,128)} %param.28) | copy-start | bytes 196612
  206.0 122.4 %all-gather.7.cloned.1.call-start = ((), (), s32[]{:S(2)}) async-start(), calls=%async_computation.3 | async-start | bytes 6635520 | tf_op jit(solution)/shard_map/all_gather | solution.py:171
  266.7 450.2 %all-reduce.22.cloned.1.call-start = ((), (), s32[]{:S(2)}) async-start(), calls=%async_computation.4 | async-start | bytes 147456 | tf_op jit(solution)/shard_map/psum | solution.py:178
  268.7 503.5 %all-reduce.24.cloned.1.call-start = ((), (), s32[]{:S(2)}) async-start(), calls=%async_computation.5 | async-start | bytes 589824 | tf_op jit(solution)/shard_map/psum | solution.py:180
  275.9 59.8 %copy-start.8 = (f32[128,128]{1,0:T(8,128)}, f32[128,128]{1,0:T(8,128)S(1)}, u32[]{:S(2)}) copy-start(f32[128,128]{1,0:T(8,128)S(1)} %fusion.19) | copy-start | bytes 196612
  340.4 2.3 copy-start.1
  703.6 69.9 %copy-start.9 = (f32[288,128]{1,0:T(8,128)S(1)}, f32[288,128]{1,0:T(8,128)}, u32[]{:S(2)}) copy-start(f32[288,128]{1,0:T(8,128)} %param.30) | copy-start | bytes 442372
  715.4 72.7 %copy-start.4 = (f32[1152,144]{0,1:T(8,128)}, f32[1152,144]{0,1:T(8,128)S(1)}, u32[]{:S(2)}) copy-start(f32[1152,144]{0,1:T(8,128)S(1)} %convolution_dynamic-update-slice_fusion.6) | copy-start | bytes 1990660
Sparse Core Ops, SparseCore 0:
  53.2 143.4 all-reduce.17
  266.8 61.6 all-gather.6
  331.9 40.6 all-reduce.21
Sparse Core Ops, SparseCore 1:
  64.7 35.0 all-gather.4
  206.1 60.5 all-reduce.19
  719.4 52.8 all-reduce.23
where the time goes:
time: 806 us; the launch traced here: 796 us
  other arithmetic  322 us (40%)
  waiting for transfers between devices  273 us (34%)
  matrix products  76.5 us (9%)
  blocking collectives  51.3 us (6%)
  local copies, waits for them, and re-layouts  49.5 us (6%)
  between operations  23.1 us (3%)
    another operation x35, other arithmetic, body(): lower = jnp.linalg.cholesky(gram)  196 us
    psum x1, waiting for transfers between devices, body(): summed_grad = lax.psum(partial_grad, ('tile', 'dp'))  132 us
    another operation x3, other arithmetic, body(): lax.linalg.triangular_solve(lower, power.T, left_side=True, lower=True)  94.4 us
    psum x1, waiting for transfers between devices, body(): lax.psum(lax.dot_general(power, power_cols, (((0,), (0,)), ((), ())), pre...  60.6 us
    psum x1, waiting for transfers between devices, body(): lax.psum((lax.dot_general(basis_cols, back, (((0,), (0,)), ((), ())), pre...  52.8 us
    another operation x27, local copies, waits for them, and re-layouts  31.4 us
    another operation x16, matrix products, body(): lower = jnp.linalg.cholesky(gram)  28.7 us
    all_gather x1, waiting for transfers between devices, body(): gram = lax.all_gather(gram_part, 'dp', axis=1, tiled=True)  28.1 us
  transfers between devices with their start and end apart: 6, of which 4 were waited for; matrix products, arithmetic and copies ran while one was open for 53% of the time, Pallas kernels for 0%

commit v1 on v0

--- a/solution.py
+++ b/solution.py
@@ -6,6 +6,27 @@
 
 highest = lax.Precision.HIGHEST
 epsilon = 1e-08
+
+
+def gather_around(x, axis, dim):
+    size, index, span = (lax.axis_size(axis), lax.axis_index(axis), x.shape[dim])
+    right = [(i, (i + 1) % size) for i in range(size)]
+    backward = [(i, (i - 1) % size) for i in range(size)]
+    whole = jnp.zeros((*x.shape[:dim], size * span, *x.shape[dim + 1 :]), x.dtype)
+    whole = lax.dynamic_update_slice_in_dim(whole, x, index * span, axis=dim)
+    from_left = from_right = x
+    half = size // 2
+    for step in range(1, half + 1):
+        from_left = lax.ppermute(from_left, axis, right)
+        whole = lax.dynamic_update_slice_in_dim(
+            whole, from_left, (index - step) % size * span, axis=dim
+        )
+        if step < size - half:
+            from_right = lax.ppermute(from_right, axis, backward)
+            whole = lax.dynamic_update_slice_in_dim(
+                whole, from_right, (index + step) % size * span, axis=dim
+            )
+    return whole
 
 
 def edge_strips(values):
@@ -168,7 +189,7 @@
     gram_part = lax.psum(
         lax.dot_general(power, power_cols, (((0,), (0,)), ((), ())), precision=highest), "tile"
     )
-    gram = lax.all_gather(gram_part, "dp", axis=1, tiled=True)
+    gram = gather_around(gram_part, "dp", 1)
     lower = jnp.linalg.cholesky(gram)
     basis_new = lax.linalg.triangular_solve(lower, power.T, left_side=True, lower=True).T
     right_new = 0.95 * right_factor + 0.05 * lax.dot_general(

time: 806 us -> 853 us (1.058)
  local copies, waits for them, and re-layouts: 49.5 us -> 72.9 us
  matrix products: 76.5 us -> 89.8 us
    ppermute x0 -> x3, waiting for transfers between devices: none -> 48.2 us  [the longest x2 38.2 us: gather_around(): from_left = lax.ppermute(from_left, axis, right)]
    all_gather x1 -> x0, waiting for transfers between devices: 28.1 us -> none  [body(): gram = lax.all_gather(gram_part, 'dp', axis=1, tiled=True)]
    dynamic_update_slice x0 -> x5, local copies, waits for them, and re-layouts: none -> 15.8 us  [the longest x3 12.2 us: gather_around(): lax.dynamic_update_slice_in_dim(whole, from_left, (index - step) % size *...]
    psum x1, waiting for transfers between devices: 60.6 us -> 47.4 us  [body(): lax.psum(lax.dot_general(power, power_cols, (((0,), (0,)), ((), ())), pre...]
    another operation x27 -> x45, local copies, waits for them, and re-layouts: 31.4 us -> 32.3 us
  transfers between devices with their start and end apart: 6 -> 8, of which waited for: 4 -> 6; matrix products, arithmetic and copies ran while one was open for 53% -> 54% of each run, Pallas kernels for 0% -> 0%
where the time goes in v1:
time: 853 us; the launch traced here: 843 us
  other arithmetic  322 us (38%)
  waiting for transfers between devices  279 us (33%)
  matrix products  89.8 us (11%)
  local copies, waits for them, and re-layouts  72.9 us (9%)
  blocking collectives  51.3 us (6%)
  between operations  23.5 us (3%)
    another operation x35, other arithmetic, body(): lower = jnp.linalg.cholesky(gram)  191 us
    psum x1, waiting for transfers between devices, body(): summed_grad = lax.psum(partial_grad, ('tile', 'dp'))  132 us
    another operation x3, other arithmetic, body(): lax.linalg.triangular_solve(lower, power.T, left_side=True, lower=True)  95.3 us
    psum x1, waiting for transfers between devices, body(): lax.psum((lax.dot_general(basis_cols, back, (((0,), (0,)), ((), ())), pre...  51.2 us
    psum x1, waiting for transfers between devices, body(): lax.psum(lax.dot_general(power, power_cols, (((0,), (0,)), ((), ())), pre...  47.4 us
    ppermute x2, waiting for transfers between devices, gather_around(): from_left = lax.ppermute(from_left, axis, right)  38.2 us
    another operation x16, matrix products, body(): lower = jnp.linalg.cholesky(gram)  34.4 us
    another operation x45, local copies, waits for them, and re-layouts  32.3 us
  transfers between devices with their start and end apart: 8, of which 6 were waited for; matrix products, arithmetic and copies ran while one was open for 54% of the time, Pallas kernels for 0%

profile of v1, /device:TPU:0, one launch (start us, length us, event | category | flops | bytes accessed | tf_op | source)
XLA Modules:
  0.0 842.7 jit_solution(18357557804776997509)
XLA Ops:
  19.2 15.8 %all_gather.16 = bf16[8,4,1,24,128]{4,3,2,1,0:T(8,128)(2,1)S(1)} all-gather(bf16[1,4,1,24,128]{4,3,2,1,0:T(8,128)(2,1)S(1)} %pad_maximum_fusion.4), channel_id=1, replica_groups=mesh['group'=1,'tile'=8,'dp'=4] {'tile'}, dimensions={0}, use_global_device_ids=true | all-gather | bytes 221184 | tf_op jit(solution)/shard_map/all_gather | solution.py:164
  36.3 14.1 %all-gather = bf16[32,1,24,128]{3,2,1,0:T(8,128)(2,1)S(1)} all-gather(bf16[4,1,24,128]{3,2,1,0:T(8,128)(2,1)S(1)} %pad_maximum_fusion.3), channel_id=2, replica_groups=mesh['group'=1,'tile'=8,'dp'=4] {'tile'}, dimensions={0}, use_global_device_ids=true | all-gather | bytes 221184 | tf_op jit(solution)/shard_map/all_gather | solution.py:151
  53.8 10.2 %all-gather.1 = bf16[4,288,144]{1,2,0:T(8,128)(2,1)S(1)} all-gather(bf16[1,288,144]{1,2,0:T(8,128)(2,1)S(1)} %bitcast_convert_fusion), channel_id=1, replica_groups=mesh['group'=1,'tile'=8,'dp'=4] {'dp'}, dimensions={0}, use_global_device_ids=true | all-gather | bytes 414720 | tf_op jit(solution)/shard_map/all_gather | solution.py:180
  65.3 132.3 %all-reduce.18.cloned.1.call-done = f32[1152,128]{1,0:T(8,128)} async-done(((f32[1152,128]{1,0:T(8,128)}), f32[1152,128]{1,0:T(8,128)}) %all-reduce.18.cloned.1.call-update) | async-done | bytes 589840 | tf_op jit(solution)/shard_map/psum | solution.py:159
  220.1 47.4 %all-reduce.20.cloned.1.call-done = f32[1152,288]{0,1:T(8,128)} async-done(((f32[1152,288]{0,1:T(8,128)}), f32[1152,288]{0,1:T(8,128)}) %all-reduce.20.cloned.1.call-update) | async-done | bytes 1327120 | tf_op jit(solution)/shard_map/psum | solution.py:189
  275.9 11.7 %cholesky.690 = f32[128,128]{1,0:T(8,128)S(1)} custom-call(f32[128,128]{1,0:T(8,128)S(1)} %fusion.108), custom_call_target="Cholesky" | custom-call | tf_op jit(solution)/shard_map/jit(cholesky)/cholesky | solution.py:103
  287.7 14.4 %collective-permute-done = f32[1152,288]{0,1:T(8,128)} collective-permute-done((f32[1152,288]{0,1:T(8,128)}, f32[1152,288]{0,1:T(8,128)}, u32[]{:S(2)}, u32[]{:S(2)}) %collective-permute-start) | collective-permute-done | bytes 1327136 | tf_op jit(solution)/shard_map/ppermute | solution.py:20
  303.7 9.8 %custom-call.85 = f32[1,128,128]{1,2,0:T(8,128)S(1)} custom-call(f32[1,128,128]{2,1,0:T(8,128)S(1)} %fusion.92), custom_call_target="InvertDiagBlocksLowerTriangular" | custom-call | tf_op jit(solution)/shard_map/triangular_solve | solution.py:104
  320.9 10.0 %collective-permute-done.1 = f32[1152,288]{0,1:T(8,128)} collective-permute-done((f32[1152,288]{0,1:T(8,128)}, f32[1152,288]{0,1:T(8,128)}, u32[]{:S(2)}, u32[]{:S(2)}) %collective-permute-start.1) | collective-permute-done | bytes 1327136 | tf_op jit(solution)/shard_map/ppermute | solution.py:25
  333.3 23.8 %collective-permute-done.2 = f32[1152,288]{0,1:T(8,128)} collective-permute-done((f32[1152,288]{0,1:T(8,128)}, f32[1152,288]{0,1:T(8,128)}, u32[]{:S(2)}, u32[]{:S(2)}) %collective-permute-start.2) | collective-permute-done | bytes 1327136 | tf_op jit(solution)/shard_map/ppermute | solution.py:20
  373.8 11.7 %cholesky.272 = f32[128,128]{1,0:T(8,128)S(1)} custom-call(f32[128,128]{1,0:T(8,128)S(1)} %cholesky.702), custom_call_target="Cholesky" | custom-call | tf_op jit(solution)/shard_map/jit(cholesky)/cholesky | solution.py:193
  385.7 9.8 %custom-call.76 = f32[1,128,128]{1,2,0:T(8,128)S(1)} custom-call(f32[1,128,128]{2,1,0:T(8,128)S(1)} %get-tuple-element.221), custom_call_target="InvertDiagBlocksLowerTriangular" | custom-call | tf_op jit(solution)/shard_map/jit(cholesky)/cholesky | solution.py:193
  399.0 11.7 %cholesky.293 = f32[128,128]{1,0:T(8,128)S(1)} custom-call(f32[128,128]{1,0:T(8,128)S(1)} %cholesky.706), custom_call_target="Cholesky" | custom-call | tf_op jit(solution)/shard_map/jit(cholesky)/cholesky | solution.py:193
  429.4 11.7 %cholesky.320 = f32[128,128]{1,0:T(8,128)S(1)} custom-call(f32[128,128]{1,0:T(8,128)S(1)} %cholesky.711), custom_call_target="Cholesky" | custom-call | tf_op jit(solution)/shard_map/jit(cholesky)/cholesky | solution.py:193
  456.8 11.7 %cholesky.581 = f32[128,128]{1,0:T(8,128)S(1)} custom-call(f32[128,128]{1,0:T(8,128)S(1)} %cholesky.716), custom_call_target="Cholesky" | custom-call | tf_op jit(solution)/shard_map/jit(cholesky)/cholesky | solution.py:193
  484.1 12.1 %cholesky.600 = f32[128,128]{1,0:T(8,128)S(1)} custom-call(f32[128,128]{1,0:T(8,128)S(1)} %cholesky.721), custom_call_target="Cholesky" | custom-call | tf_op jit(solution)/shard_map/jit(cholesky)/cholesky | solution.py:193
  511.7 11.7 %cholesky.620 = f32[128,128]{1,0:T(8,128)S(1)} custom-call(f32[128,128]{1,0:T(8,128)S(1)} %cholesky.726), custom_call_target="Cholesky" | custom-call | tf_op jit(solution)/shard_map/jit(cholesky)/cholesky | solution.py:193
  538.8 11.7 %cholesky.640 = f32[128,128]{1,0:T(8,128)S(1)} custom-call(f32[128,128]{1,0:T(8,128)S(1)} %cholesky.731), custom_call_target="Cholesky" | custom-call | tf_op jit(solution)/shard_map/jit(cholesky)/cholesky | solution.py:193
  565.1 11.9 %cholesky.660 = f32[128,128]{1,0:T(8,128)S(1)} custom-call(f32[128,128]{1,0:T(8,128)S(1)} %cholesky.736), custom_call_target="Cholesky" | custom-call | tf_op jit(solution)/shard_map/jit(cholesky)/cholesky | solution.py:193
  590.8 11.7 %cholesky.678 = f32[128,128]{1,0:T(8,128)S(1)} custom-call(f32[128,128]{1,0:T(8,128)S(1)} %slice_subtract_fusion.7), custom_call_target="Cholesky" | custom-call | tf_op jit(solution)/shard_map/jit(cholesky)/cholesky | solution.py:193
  620.1 32.4 %while.5 = (s32[]{:T(128)}, f32[1152,1152]{0,1:T(8,128)}, s32[9,2]{0,1:T(2,128)S(1)}, f32[9,128,128]{2,1,0:T(8,128)}, s32[]{:T(128)}) while((s32[]{:T(128)}, f32[1152,1152]{0,1:T(8,128)}, s32[9,2]{0,1:T(2,128)S(1)}, f32[9,128,128]{2,1,0:T(8,128)}, s32[]{:T(128)}) %tuple.108), condition=%wide.while_cond.4, body=%wide.while_body.4.sunk | while | flops 2 | bytes 393329 | solution.py:194
  652.5 90.1 %custom-call.84 = f32[9,128,128]{1,2,0:T(8,128)} custom-call(f32[9,128,128]{2,1,0:T(8,128)} %get-tuple-element.65), custom_call_target="InvertDiagBlocksLowerTriangular" | custom-call | tf_op jit(solution)/shard_map/triangular_solve | solution.py:194
  767.6 51.2 %all-reduce.24.cloned.1.call-done = (f32[288,128]{1,0:T(8,128)}, f32[288,128]{1,0:T(8,128)}) async-done(((f32[288,128]{1,0:T(8,128)}, f32[288,128]{1,0:T(8,128)}), (f32[288,128]{1,0:T(8,128)}, f32[288,128]{1,0:T(8,128)})) %all-reduce.24.cloned.1.call-update) | async-done | bytes 294928 | tf_op jit(solution)/shard_map/psum | solution.py:201
  821.9 11.2 %all_gather.19 = f32[1152,128]{1,0:T(8,128)S(1)} all-gather(f32[288,128]{1,0:T(8,128)S(1)} %get-tuple-element.148), channel_id=1, replica_groups=mesh['group'=1,'tile'=8,'dp'=4] {'dp'}, dimensions={0}, use_global_device_ids=true | all-gather | bytes 737280 | tf_op jit(solution)/shard_map/all_gather | solution.py:216
  (272 shorter events, 261.4 us)
Async XLA Ops:
  8.0 1.0 copy-start
  8.0 27.8 %copy-start.14 = (s32[4]{0:T(128)S(1)}, s32[4]{0:T(128)}, u32[]{:S(2)}) copy-start(s32[4]{0:T(128)} %constant.547.clone) | copy-start | bytes 52
  8.0 11.1 %copy-start.5 = (bf16[1,1,24,24,128]{4,3,2,1,0:T(8,128)(2,1)S(1)}, bf16[1,1,24,24,128]{4,3,2,1,0:T(8,128)(2,1)}, u32[]{:S(2)}) copy-start(bf16[1,1,24,24,128]{4,3,2,1,0:T(8,128)(2,1)} %param.20) | copy-start | bytes 442372
  8.0 27.6 %copy-start.13 = (s32[1,4]{1,0:T(1,128)S(1)}, s32[1,4]{1,0:T(1,128)}, u32[]{:S(2)}) copy-start(s32[1,4]{1,0:T(1,128)} %param.24) | copy-start | bytes 52
  8.1 189.5 %all-reduce.18.cloned.1.call-start = ((), (), s32[]{:S(2)}) async-start(), calls=%async_computation | async-start | bytes 1179648 | tf_op jit(solution)/shard_map/psum | solution.py:159
  19.1 34.7 %copy-start.7 = (f32[144,288]{1,0:T(8,128)S(1)}, f32[144,288]{1,0:T(8,128)}, u32[]{:S(2)}) copy-start(f32[144,288]{1,0:T(8,128)} %param.26) | copy-start | bytes 497668
  53.7 147.1 %all-gather.4.cloned.1.call-start = ((), (), s32[]{:S(2)}) async-start(), calls=%async_computation.1 | async-start | bytes 2985984 | tf_op jit(solution)/shard_map/all_gather | solution.py:183
  65.2 202.3 %all-reduce.20.cloned.1.call-start = ((), (), s32[]{:S(2)}) async-start(), calls=%async_computation.2 | async-start | bytes 2654208 | tf_op jit(solution)/shard_map/psum | solution.py:189
  198.7 564.9 %copy-start.2 = (f32[1152,128]{1,0:T(8,128)}, f32[1152,128]{1,0:T(8,128)S(1)}, u32[]{:S(2)}) copy-start(f32[1152,128]{1,0:T(8,128)S(1)} %broadcast_multiply_fusion) | copy-start | bytes 1769476
  198.7 12.3 %copy-start.11 = (f32[4,1,24,128]{3,2,1,0:T(8,128)S(1)}, f32[4,1,24,128]{3,2,1,0:T(8,128)}, u32[]{:S(2)}) copy-start(f32[4,1,24,128]{3,2,1,0:T(8,128)} %get-tuple-element.228) | copy-start | bytes 147460
  200.8 70.6 %copy-start.3 = (f32[144,1152]{1,0:T(8,128)}, f32[144,1152]{1,0:T(8,128)S(1)}, u32[]{:S(2)}) copy-start(f32[144,1152]{1,0:T(8,128)S(1)} %fusion.1) | copy-start | bytes 1990660
  204.4 69.0 %copy-start.8 = (f32[128,128]{1,0:T(8,128)S(1)}, f32[128,128]{1,0:T(8,128)}, u32[]{:S(2)}) copy-start(f32[128,128]{1,0:T(8,128)} %param.28) | copy-start | bytes 196612
  207.0 558.1 %all-reduce.22.cloned.1.call-start = ((), (), s32[]{:S(2)}) async-start(), calls=%async_computation.3 | async-start | bytes 147456 | tf_op jit(solution)/shard_map/psum | solution.py:199
  209.0 609.8 %all-reduce.24.cloned.1.call-start = ((), (), s32[]{:S(2)}) async-start(), calls=%async_computation.4 | async-start | bytes 589824 | tf_op jit(solution)/shard_map/psum | solution.py:201
  267.5 34.6 %collective-permute-start = (f32[1152,288]{0,1:T(8,128)}, f32[1152,288]{0,1:T(8,128)}, u32[]{:S(2)}, u32[]{:S(2)}) collective-permute-start(f32[1152,288]{0,1:T(8,128)} %all-reduce.20.cloned.1.call-done), channel_id=1, source_target_pairs={{0,1},{1,2},{2,3},{3,0},{4,5},{5,6},{6,7},{7,4},{8,9},{9,10},{10,1... | collective-permute-start | bytes 3981320 | tf_op jit(solution)/shard_map/ppermute | solution.py:20
  271.3 45.9 %copy-start.6 = (f32[1152,288]{0,1:T(8,128)S(1)}, f32[1152,288]{0,1:T(8,128)}, u32[]{:S(2)}) copy-start(f32[1152,288]{0,1:T(8,128)} %all-reduce.20.cloned.1.call-done) | copy-start | bytes 3981316
  273.4 0.6 copy-start.10
  274.4 56.4 %collective-permute-start.1 = (f32[1152,288]{0,1:T(8,128)}, f32[1152,288]{0,1:T(8,128)}, u32[]{:S(2)}, u32[]{:S(2)}) collective-permute-start(f32[1152,288]{0,1:T(8,128)} %all-reduce.20.cloned.1.call-done), channel_id=1, source_target_pairs={{0,3},{1,0},{2,1},{3,2},{4,7},{5,4},{6,5},{7,6},{8,11},{9,8},{10,9... | collective-permute-start | bytes 3981320 | tf_op jit(solution)/shard_map/ppermute | solution.py:25
  302.1 55.1 %collective-permute-start.2 = (f32[1152,288]{0,1:T(8,128)}, f32[1152,288]{0,1:T(8,128)}, u32[]{:S(2)}, u32[]{:S(2)}) collective-permute-start(f32[1152,288]{0,1:T(8,128)} %collective-permute-done), channel_id=1, source_target_pairs={{0,1},{1,2},{2,3},{3,0},{4,5},{5,6},{6,7},{7,4},{8,9},{9,10},{10,1... | collective-permute-start | bytes 3981320 | tf_op jit(solution)/shard_map/ppermute | solution.py:20
  371.5 2.3 copy-start.1
  744.7 22.7 %copy-start.9 = (f32[128,128]{1,0:T(8,128)S(1)}, f32[128,128]{1,0:T(8,128)}, u32[]{:S(2)}) copy-start(f32[128,128]{1,0:T(8,128)} %param.28) | copy-start | bytes 196612
  745.8 74.2 %copy-start.12 = (f32[288,128]{1,0:T(8,128)S(1)}, f32[288,128]{1,0:T(8,128)}, u32[]{:S(2)}) copy-start(f32[288,128]{1,0:T(8,128)} %param.30) | copy-start | bytes 442372
  763.6 71.1 %copy-start.4 = (f32[1152,144]{0,1:T(8,128)}, f32[1152,144]{0,1:T(8,128)S(1)}, u32[]{:S(2)}) copy-start(f32[1152,144]{0,1:T(8,128)S(1)} %convolution_dynamic-update-slice_fusion.6) | copy-start | bytes 1990660
Sparse Core Ops, SparseCore 0:
  53.8 143.7 all-reduce.17
Sparse Core Ops, SparseCore 1:
  65.3 35.1 all-gather.3
  207.0 60.4 all-reduce.19
  270.9 40.9 all-reduce.21
  767.5 51.2 all-reduce.23
